TPU v7x, 256 devices: a whole 4x4x8 slice. The times are simulated.
256 devices in a mesh: row: 32 (over z_lo, x, core), col: 8 (over z_hi, y).
Axes of the slice: x: 4, y: 4, z: 8 (z_hi: 2, z_lo: 4; z = z_hi * 4 + z_lo), core: 2. Of those that a mesh axis runs over, the one named last changes fastest.
Arguments:
- pair: bfloat16 [512, 512, 128], P('row', 'col'), may hold values from -6 to 6
- cotangent: bfloat16 [64, 512, 512], P(None, 'row', 'col'), may hold values from -0.59765625 to 0.59765625
- w_left: bfloat16 [128, 64], replicated, may hold values from -0.5 to 0.5
- w_left_gate: bfloat16 [128, 64], replicated, may hold values from -0.5 to 0.5
- w_right: bfloat16 [128, 64], replicated, may hold values from -0.5 to 0.5
- w_right_gate: bfloat16 [128, 64], replicated, may hold values from -0.5 to 0.5
Outputs:
- pair_gradient: bfloat16 [512, 512, 128], P('row', 'col')
- grad_left: float32 [128, 64], replicated
- grad_left_gate: float32 [128, 64], replicated
- grad_right: float32 [128, 64], replicated
- grad_right_gate: float32 [128, 64], replicated
All inputs are finite; a program needn't handle non-finite values.
Results may differ from a plain program's by a relative error of at most 0.0082.
Values may be sent and summed in bfloat16 or wider, within the bound.
A program may use at most 64 MiB of HBM per device.

v0:
```python
import jax
import jax.numpy as jnp
from jax import lax
from jax.sharding import PartitionSpec as P


def shards(pair, cotangent, w_left, w_left_gate, w_right, w_right_gate):
    pair_f = pair.astype(jnp.float32)
    average = jnp.mean(pair_f, axis=-1, keepdims=True)
    centered_input = pair_f - average
    variance = jnp.mean(centered_input * centered_input, axis=-1, keepdims=True)
    inverse_scale = 1.0 / jnp.sqrt(variance + 1e-05)
    standardized_input = centered_input * inverse_scale
    normalized_input = standardized_input.astype(jnp.bfloat16)
    stacked = jnp.concatenate([w_left, w_left_gate, w_right, w_right_gate], axis=1)
    projected = jnp.einsum(
        "rcd,dh->hrc", normalized_input, stacked, preferred_element_type=jnp.float32
    )
    q_left, p_left, q_right, p_right = jnp.split(projected, 4, axis=0)
    s_left = jax.nn.sigmoid(p_left)
    s_right = jax.nn.sigmoid(p_right)
    left = (s_left * q_left).astype(jnp.bfloat16)
    right = (s_right * q_right).astype(jnp.bfloat16)
    g_chan, left_chan, right_chan = (
        lax.all_to_all(cotangent, "col", split_axis=0, concat_axis=2, tiled=True),
        lax.all_to_all(left, "col", split_axis=0, concat_axis=2, tiled=True),
        lax.all_to_all(right, "col", split_axis=0, concat_axis=2, tiled=True),
    )
    residues = g_chan.shape[2]
    col_block = g_chan
    d_left = jnp.einsum(
        "hij,hjk->hik",
        col_block,
        lax.all_gather(right_chan, "row", axis=1, tiled=True),
        preferred_element_type=jnp.float32,
    )
    col_block = g_chan
    summed = lax.psum_scatter(
        jnp.einsum("hij,hik->jhk", col_block, left_chan, preferred_element_type=jnp.float32),
        "row",
        scatter_dimension=0,
        tiled=True,
    )
    d_right = jnp.transpose(summed, (1, 0, 2))
    d_left_tile, d_right_tile = (
        lax.all_to_all(d_left.astype(jnp.bfloat16), "col", split_axis=2, concat_axis=0, tiled=True),
        lax.all_to_all(
            d_right.astype(jnp.bfloat16), "col", split_axis=2, concat_axis=0, tiled=True
        ),
    )
    grad_l = d_left_tile.astype(jnp.float32)
    grad_r = d_right_tile.astype(jnp.float32)
    e_left = grad_l * s_left
    f_left = grad_l * q_left * s_left * (1.0 - s_left)
    e_right = grad_r * s_right
    f_right = grad_r * q_right * s_right * (1.0 - s_right)
    grads = jnp.concatenate([e_left, f_left, e_right, f_right], axis=0).astype(jnp.bfloat16)
    local_weights = jnp.einsum(
        "rcd,hrc->dh", normalized_input, grads, preferred_element_type=jnp.float32
    )
    total_weights = lax.psum(local_weights, ("row", "col")) / residues
    normalized_gradient = jnp.einsum(
        "hrc,dh->rcd", grads, stacked, preferred_element_type=jnp.float32
    )
    gradient_mean = jnp.mean(normalized_gradient, axis=-1, keepdims=True)
    gradient_input_mean = jnp.mean(normalized_gradient * standardized_input, axis=-1, keepdims=True)
    pair_gradient = (
        (normalized_gradient - gradient_mean - standardized_input * gradient_input_mean)
        * inverse_scale
    ).astype(jnp.bfloat16)
    pieces_w = jnp.split(total_weights, 4, axis=1)
    return (pair_gradient, pieces_w[0], pieces_w[1], pieces_w[2], pieces_w[3])


def solution(mesh):
    in_specs = (P("row", "col", None), P(None, "row", "col"), P(), P(), P(), P())
    out_specs = (P("row", "col", None), P(), P(), P(), P())
    return jax.shard_map(shards, mesh=mesh, in_specs=in_specs, out_specs=out_specs, check_vma=False)
```

profile of v0, /device:TPU:1, one launch (start us, length us, event | category | flops | bytes accessed | tf_op | source)
XLA Modules:
  0.0 579.4 jit_solution(9537658770375944991)
XLA Ops:
  7.2 1.2 convert_reduce_fusion
  8.4 1.3 fusion.10
  9.8 0.8 copy.87
  10.6 0.8 copy.88
  11.4 0.8 copy.89
  12.3 0.8 copy.90
  13.1 1.4 fusion.18
  14.6 0.2 multiply_convert_fusion.5
  14.8 0.3 copy.91
  15.1 0.2 reshape.47
  15.3 20.8 %all_to_all.72 = bf16[8,2,4096]{2,1,0:T(2,128)(2,1)S(1)} all-to-all(bf16[8,2,4096]{2,1,0:T(2,128)(2,1)S(1)} %reshape.47), channel_id=1, replica_groups=mesh['row'=32,'col'=8] {'col'}, dimensions={0} | all-to-all | bytes 262144 | tf_op jit(solution)/shard_map/all_to_all | solution.py:27
  36.5 0.9 all_to_all.56
  37.4 0.2 reshape.45
  37.7 11.9 %all_to_all.73 = bf16[8,2,4096]{2,1,0:T(2,128)(2,1)S(1)} all-to-all(bf16[8,2,4096]{2,1,0:T(2,128)(2,1)S(1)} %reshape.45), channel_id=1, replica_groups=mesh['row'=32,'col'=8] {'col'}, dimensions={0} | all-to-all | bytes 262144 | tf_op jit(solution)/shard_map/all_to_all | solution.py:25
  50.0 0.2 all_to_all.60
  50.2 47.2 %all-gather.2.cloned.1.call-done = bf16[8,512,512]{2,1,0:T(8,128)(2,1)} async-done(((bf16[8,16,512]{2,1,0:T(8,128)(2,1)}), bf16[8,512,512]{2,1,0:T(8,128)(2,1)}) %all-gather.2.cloned.1.call-update) | async-done | bytes 4194320 | tf_op jit(solution)/shard_map/all_gather | solution.py:34
  97.4 2.8 fusion
  100.2 0.8 copy.94
  101.0 1.1 reshape.49
  102.0 16.9 %all_to_all.74 = bf16[8,2,4096]{2,1,0:T(2,128)(2,1)S(1)} all-to-all(bf16[8,2,4096]{2,1,0:T(2,128)(2,1)S(1)} %reshape.49), channel_id=1, replica_groups=mesh['row'=32,'col'=8] {'col'}, dimensions={0} | all-to-all | bytes 262144 | tf_op jit(solution)/shard_map/all_to_all | solution.py:46
  118.9 0.7 reshape.50
  119.7 0.7 copy.95
  120.6 0.3 copy.97
  120.9 0.4 multiply_convert_fusion.4
  121.3 0.3 copy.99
  121.5 0.2 reshape.51
  121.8 11.9 %all_to_all.75 = bf16[8,2,4096]{2,1,0:T(2,128)(2,1)S(1)} all-to-all(bf16[8,2,4096]{2,1,0:T(2,128)(2,1)S(1)} %reshape.51), channel_id=1, replica_groups=mesh['row'=32,'col'=8] {'col'}, dimensions={0} | all-to-all | bytes 262144 | tf_op jit(solution)/shard_map/all_to_all | solution.py:26
  134.0 0.2 all_to_all.65
  134.2 4.5 convolution_bitcast_fusion
  138.7 10.4 %copy.101 = f32[512,8,512]{2,1,0:T(8,128)} copy(f32[512,8,512]{0,2,1:T(8,128)} %convolution_bitcast_fusion) | data formatting | bytes 16777216 | tf_op jit(solution)/shard_map/hij,hik->jhk/transpose | solution.py:39
  149.3 152.1 %reduce-scatter.2.cloned.1.call-done = f32[16,8,512]{2,1,0:T(8,128)} async-done(((f32[512,8,512]{2,1,0:T(8,128)}), f32[16,8,512]{2,1,0:T(8,128)}) %reduce-scatter.2.cloned.1.call-update) | async-done | bytes 262160 | tf_op jit(solution)/shard_map/reduce_scatter | solution.py:38
  301.4 1.0 convert_bitcast_fusion
  302.4 0.8 copy.102
  303.2 1.1 reshape.53
  304.3 18.0 %all_to_all.76 = bf16[8,2,4096]{2,1,0:T(2,128)(2,1)S(1)} all-to-all(bf16[8,2,4096]{2,1,0:T(2,128)(2,1)S(1)} %reshape.53), channel_id=1, replica_groups=mesh['row'=32,'col'=8] {'col'}, dimensions={0} | all-to-all | bytes 262144 | tf_op jit(solution)/shard_map/all_to_all | solution.py:47
  322.2 0.7 reshape.54
  322.9 0.7 copy.103
  323.9 0.3 copy.105
  324.2 0.3 multiply_convert_fusion.1
  324.5 1.5 convolution_bitcast_fusion.1
  326.0 1.0 fusion.21
  327.1 1.3 fusion.9
  328.4 240.6 %all-reduce.2.cloned.1.call-done = f32[128,256]{1,0:T(8,128)} async-done(((f32[128,256]{1,0:T(8,128)}), f32[128,256]{1,0:T(8,128)}) %all-reduce.2.cloned.1.call-update) | async-done | bytes 131088 | tf_op jit(solution)/shard_map/psum | solution.py:61
  569.0 0.9 broadcast_multiply_fusion
  570.0 0.7 copy.110
  570.8 0.7 copy.109
  571.5 0.7 copy.108
  572.1 0.7 copy.107
  (24 shorter events, 1.9 us)
Async XLA Ops:
  7.2 30.3 %copy-start.1 = (bf16[64,16,64]{2,1,0:T(8,128)(2,1)S(1)}, bf16[64,16,64]{2,1,0:T(8,128)(2,1)}, u32[]{:S(2)}) copy-start(bf16[64,16,64]{2,1,0:T(8,128)(2,1)} %param.7) | copy-start | bytes 393220
  7.2 90.2 %all-gather.2.cloned.1.call-start = ((), (), s32[]{:S(2)}) async-start(), calls=%async_computation.6 | async-start | bytes 4325376 | tf_op jit(solution)/shard_map/all_gather | solution.py:34
  37.4 264.0 %reduce-scatter.2.cloned.1.call-start = ((), (), s32[]{:S(2)}) async-start(), calls=%async_computation.7 | async-start | bytes 8650752 | tf_op jit(solution)/shard_map/reduce_scatter | solution.py:38
  149.2 419.8 %all-reduce.2.cloned.1.call-start = ((), (), s32[]{:S(2)}) async-start(), calls=%async_computation.8 | async-start | bytes 262144 | tf_op jit(solution)/shard_map/psum | solution.py:61
  303.2 21.3 %copy-start = (bf16[16,64,128]{2,1,0:T(8,128)(2,1)S(1)}, bf16[16,64,128]{2,1,0:T(8,128)(2,1)}, u32[]{:S(2)}) copy-start(bf16[16,64,128]{2,1,0:T(8,128)(2,1)} %param.6) | copy-start | bytes 786436
Sparse Core Ops, SparseCore 0:
  37.5 59.8 all-gather.1
  149.3 152.0 reduce-scatter.1
  327.2 241.8 all-reduce.1
where the time goes:
time: 581 us; the launch traced here: 579 us
  waiting for transfers between devices  440 us (76%)
  blocking collectives  79.4 us (14%)
  local copies, waits for them, and re-layouts  27.9 us (5%)
  between operations  14 us (2%)
  matrix products  11.3 us (2%)
  other arithmetic  6.66 us (1%)
    psum x1, waiting for transfers between devices, shards(): total_weights = lax.psum(local_weights, ('row', 'col')) / residues  241 us
    reduce_scatter x1, waiting for transfers between devices, shards(): lax.psum_scatter(jnp.einsum('hij,hik->jhk', col_block, left_chan, preferr...  152 us
    all_gather x1, waiting for transfers between devices, shards(): lax.all_gather(right_chan, 'row', axis=1, tiled=True)  47.2 us
    all_to_all x1, blocking collectives, shards(): lax.all_to_all(right, 'col', split_axis=0, concat_axis=2, tiled=True)  20.8 us
    all_to_all x1, blocking collectives, shards(): lax.all_to_all(d_right.astype(jnp.bfloat16), 'col', split_axis=2, concat_...  18 us
    all_to_all x1, blocking collectives, shards(): lax.all_to_all(d_left.astype(jnp.bfloat16), 'col', split_axis=2, concat_a...  16.9 us
    all_to_all x1, blocking collectives, shards(): lax.all_to_all(cotangent, 'col', split_axis=0, concat_axis=2, tiled=True)  11.9 us
    all_to_all x1, blocking collectives, shards(): lax.all_to_all(left, 'col', split_axis=0, concat_axis=2, tiled=True)  11.9 us
  transfers between devices with their start and end apart: 3, of which 3 were waited for; matrix products, arithmetic and copies ran while one was open for 0% of the time, Pallas kernels for 0%

commit v1 on v0

v1 whole, which is shorter than its diff:
```python
import jax
import jax.numpy as jnp
from jax import lax
from jax.experimental import pallas as pl
from jax.experimental.pallas import tpu as pltpu
from jax.sharding import PartitionSpec as P

MESH = pl.DeviceIdType.MESH
BF, F32 = jnp.bfloat16, jnp.float32


def swap(v):
    return pltpu.roll(v, 64, v.ndim - 1)


def kernel(
    pair_hbm, cot_hbm, wl, wlg, wr, wrg,
    pg_out, o_l, o_lg, o_r, o_rg,
    pair_v, cot_v, wst, wcat, xhat, invs, scr, s_s, f_s, nblk,
    gs, gb, gg, lrs, lrb, dsd, db, efs, ws, rb, yb, ag,
    load_sem, send_sem, recv_sem,
):
    row, col = lax.axis_index("row"), lax.axis_index("col")
    zhi, y = lax.div(col, 4), lax.rem(col, 4)
    me = zhi * 32 + row
    core, chip = lax.rem(row, 2), lax.div(me, 2)

    def member(g):
        return (lax.rem(g, 32), lax.div(g, 32) * 4 + y)

    def other_y(d):
        return (row, zhi * 4 + lax.rem(y + d, 4))

    def remote(src, dst, phase, device):
        return pltpu.make_async_remote_copy(
            src_ref=src, dst_ref=dst, send_sem=send_sem.at[phase], recv_sem=recv_sem.at[phase],
            device_id=device, device_id_type=MESH,
        )

    load_pair = pltpu.make_async_copy(pair_hbm, pair_v, load_sem.at[0])
    load_cot = pltpu.make_async_copy(cot_hbm, cot_v, load_sem.at[1])
    load_cot.start()
    load_pair.start()

    barrier = pltpu.get_barrier_semaphore()

    def greet(d, c):
        pl.semaphore_signal(
            barrier, inc=1, device_id=member(lax.rem(me + d, 64)), device_id_type=MESH
        )
        return c

    lax.fori_loop(1, 64, greet, 0)
    for d in (1, 2, 3):
        pl.semaphore_signal(barrier, inc=1, device_id=other_y(d), device_id_type=MESH)

    wst[0:64], wst[64:128], wst[128:192], wst[192:256] = wl[...], wlg[...], wr[...], wrg[...]
    wcat[0:64, 0:128], wcat[0:64, 128:256] = wr[...], wl[...]
    wcat[64:128, 0:128], wcat[64:128, 128:256] = wrg[...], wlg[...]

    load_cot.wait()

    def pack(t, c):
        g = cot_v[pl.ds(t * 8, 8)].astype(F32)
        gs[pl.ds(t * 8, 8)] = jnp.concatenate([g[:, :8], g[:, 8:]], axis=-1).astype(BF)
        return c

    lax.fori_loop(0, 8, pack, 0)
    load_pair.wait()

    low = lax.broadcasted_iota(jnp.int32, (64, 128), 1) < 64

    def project(b, c):
        x = pair_v[pl.ds(2 * b, 2)].astype(F32).reshape(128, 128)
        cen = x - jnp.mean(x, axis=1, keepdims=True)
        var = jnp.mean(cen * cen, axis=1, keepdims=True)
        inv = jnp.broadcast_to(1.0 / jnp.sqrt(var + 1e-05), (128, 128))
        xh = cen * inv
        xhat[pl.ds(128 * b, 128)] = xh
        invs[pl.ds(128 * b, 128)] = inv
        pt = lax.dot_general(
            wst[...], xh.astype(BF), (((1,), (1,)), ((), ())), preferred_element_type=F32
        )
        q_l, p_l, q_r, p_r = pt[0:64], pt[64:128], pt[128:192], pt[192:256]
        s_l, s_r = jax.nn.sigmoid(p_l), jax.nn.sigmoid(p_r)
        l, r = s_l * q_l, s_r * q_r
        f_l, f_r = l * (1.0 - s_l), r * (1.0 - s_r)
        scr[pl.ds(2 * b, 64, stride=16), :] = jnp.where(low, l, swap(r))
        scr[pl.ds(2 * b + 1, 64, stride=16), :] = jnp.where(low, swap(l), r)
        s_lw, s_rw, f_lw, f_rw = swap(s_l), swap(s_r), swap(f_l), swap(f_r)
        s_s[2 * b], s_s[2 * b + 1] = jnp.where(low, s_r, s_lw), jnp.where(low, s_rw, s_l)
        f_s[2 * b], f_s[2 * b + 1] = jnp.where(low, f_r, f_lw), jnp.where(low, f_rw, f_l)
        return c

    lax.fori_loop(0, 8, project, 0)

    def round_lr(t, c):
        v = scr[pl.ds(t * 128, 128), :]
        lrs[pl.ds(t * 8, 8)] = v.reshape(8, 16, 128).astype(BF)
        return c

    lax.fori_loop(0, 8, round_lr, 0)

    pl.semaphore_wait(barrier, 66)

    def scatter(src, dst, phase):
        def step(d, c):
            g = lax.rem(me + d, 64)
            remote(src.at[g], dst, phase, member(g)).start()
            return c

        lax.fori_loop(1, 64, step, 0)

    scatter(gs, gb.at[y, me], 0)
    gb[y, me] = gs[me]
    scatter(lrs, lrb.at[me], 1)
    lrb[me] = lrs[me]

    def spread(b, c):
        n = xhat[pl.ds(128 * b, 128), :].astype(BF)
        z = jnp.zeros((64, 128), BF)
        nblk[pl.ds(256 * b, 256), 0:128] = jnp.concatenate([n[:64], z, n[64:], z], axis=0)
        nblk[pl.ds(256 * b, 256), 128:256] = jnp.concatenate([z, n[:64], z, n[64:]], axis=0)
        return c

    lax.fori_loop(0, 8, spread, 0)

    remote(gs.at[pl.ds(0, 63)], gb.at[0, pl.ds(0, 63)], 0, other_y(1)).wait_recv()
    for d in (1, 2, 3):
        remote(gb.at[y], gb.at[y], 2, other_y(d)).start()
    remote(gb.at[pl.ds(0, 3)], gb.at[pl.ds(0, 3)], 2, other_y(1)).wait_recv()

    low3 = lax.broadcasted_iota(jnp.int32, (8, 8, 128), 2) < 64
    for t in range(4):
        for q in range(4):
            src = pl.ds((q // 2) * 32 + 8 * t, 8)
            a = gb[2 * (q % 2), src].astype(F32)
            b = gb[2 * (q % 2) + 1, src].astype(F32)
            top, bottom = jnp.where(low3, a, swap(b)), jnp.where(low3, swap(a), b)
            full = jnp.stack([top, bottom], axis=1).reshape(128, 128)
            gg[t * 128 : t * 128 + 128, q * 128 : q * 128 + 128] = full.astype(BF)
            gg[512 + q * 128 : 640 + q * 128, t * 128 : t * 128 + 128] = full.T.astype(BF)

    remote(lrs.at[pl.ds(0, 63)], lrb.at[pl.ds(0, 63)], 1, other_y(1)).wait_recv()
    both = jnp.concatenate(
        [lrb[0:32].reshape(512, 128), lrb[32:64].reshape(512, 128)], axis=1
    )
    low2 = lax.broadcasted_iota(jnp.int32, (128, 128), 1) < 64
    for m in range(4):
        d_l = jnp.dot(gg[128 * m : 128 * m + 128], both, preferred_element_type=F32)
        d_r = jnp.dot(gg[512 + 128 * m : 640 + 128 * m], both, preferred_element_type=F32)
        for z in range(2):
            lanes = slice(128 * z, 128 * z + 128)
            d = jnp.where(low2, d_r[:, lanes], d_l[:, lanes])
            dsd[32 * z + 8 * m : 32 * z + 8 * m + 8] = d.reshape(8, 16, 128).astype(BF)

    scatter(dsd, db.at[me], 3)
    db[me] = dsd[me]
    remote(dsd.at[pl.ds(0, 63)], db.at[pl.ds(0, 63)], 3, other_y(1)).wait_recv()

    def widen(t, c):
        scr[pl.ds(t * 128, 128), :] = db[pl.ds(t * 8, 8)].astype(F32).reshape(128, 128)
        return c

    lax.fori_loop(0, 8, widen, 0)
    for i in range(16):
        d = scr[pl.ds(i, 64, stride=16), :]
        efs[0:64, 128 * i : 128 * i + 128] = (d * s_s[i]).astype(BF)
        efs[64:128, 128 * i : 128 * i + 128] = (d * f_s[i]).astype(BF)
    wg = jnp.dot(efs[...], nblk[...], preferred_element_type=F32)
    ws[0:16] = wg[:, 0:128].reshape(16, 8, 128)
    ws[16:32] = wg[:, 128:256].reshape(16, 8, 128)

    def reduce_to(d, c):
        t = lax.rem(chip + d, 32)
        remote(ws.at[t], rb.at[me], 4, member(2 * t)).start()
        return c

    lax.fori_loop(1, 32, reduce_to, 0)

    @pl.when(core == 1)
    def _():
        remote(ws.at[chip], rb.at[me], 4, member(2 * chip)).start()

    @pl.when(core == 0)
    def _():
        rb[me] = ws[chip]

    for b in range(8):
        part = lax.dot_general(
            efs[:, 256 * b : 256 * b + 256], wcat[...], (((0,), (0,)), ((), ())),
            preferred_element_type=F32,
        )
        dn = jnp.concatenate(
            [
                part[0:64, 0:128] + part[64:128, 128:256],
                part[128:192, 0:128] + part[192:256, 128:256],
            ],
            axis=0,
        )
        xh = xhat[128 * b : 128 * b + 128, :]
        m1 = jnp.mean(dn, axis=1, keepdims=True)
        m2 = jnp.mean(dn * xh, axis=1, keepdims=True)
        pg = (dn - m1 - xh * m2) * invs[128 * b : 128 * b + 128, :]
        pg_out[2 * b : 2 * b + 2] = pg.reshape(2, 64, 128).astype(BF)

    @pl.when(core == 0)
    def _():
        remote(rb.at[pl.ds(0, 63)], rb.at[pl.ds(0, 63)], 4, other_y(1)).wait_recv()
        yb[y] = jnp.sum(rb[...], axis=0)
        for d in (1, 2, 3):
            remote(yb.at[y], yb.at[y], 5, other_y(d)).start()
        remote(yb.at[pl.ds(0, 3)], yb.at[pl.ds(0, 3)], 5, other_y(1)).wait_recv()
        ag[chip] = ((yb[0] + yb[1]) + (yb[2] + yb[3])) * (1.0 / 512)

        def share(d, c):
            remote(ag.at[chip], ag.at[chip], 6, member(lax.rem(me + d, 64))).start()
            return c

        lax.fori_loop(1, 64, share, 0)
        remote(ag.at[pl.ds(0, 31)], ag.at[pl.ds(0, 31)], 6, other_y(1)).wait_recv()
        remote(rb.at[pl.ds(0, 63)], rb.at[pl.ds(0, 63)], 6, other_y(1)).wait_send()
        remote(yb.at[pl.ds(0, 3)], yb.at[pl.ds(0, 3)], 5, other_y(1)).wait_send()
        remote(ws.at[pl.ds(0, 31)], ws.at[pl.ds(0, 31)], 4, other_y(1)).wait_send()

    @pl.when(core == 1)
    def _():
        remote(ag, ag, 6, other_y(1)).wait_recv()
        remote(ws, ws, 4, other_y(1)).wait_send()

    o_r[...] = ag[0:8].reshape(64, 128)
    o_rg[...] = ag[8:16].reshape(64, 128)
    o_l[...] = ag[16:24].reshape(64, 128)
    o_lg[...] = ag[24:32].reshape(64, 128)

    remote(gs.at[pl.ds(0, 63)], gs.at[pl.ds(0, 63)], 0, other_y(1)).wait_send()
    remote(lrs.at[pl.ds(0, 63)], lrs.at[pl.ds(0, 63)], 1, other_y(1)).wait_send()
    remote(gb.at[pl.ds(0, 3)], gb.at[pl.ds(0, 3)], 2, other_y(1)).wait_send()
    remote(dsd.at[pl.ds(0, 63)], dsd.at[pl.ds(0, 63)], 3, other_y(1)).wait_send()


def shards(pair, cotangent, w_left, w_left_gate, w_right, w_right_gate):
    vm = pltpu.VMEM
    grad = jax.ShapeDtypeStruct((64, 128), F32)
    pg, g_l, g_lg, g_r, g_rg = pl.pallas_call(
        kernel,
        out_shape=[jax.ShapeDtypeStruct((16, 64, 128), BF), grad, grad, grad, grad],
        in_specs=[pl.BlockSpec(memory_space=pl.ANY)] * 2 + [pl.BlockSpec(memory_space=vm)] * 4,
        out_specs=[pl.BlockSpec(memory_space=vm)] * 5,
        scratch_shapes=[
            vm((16, 64, 128), BF),
            vm((64, 16, 64), BF),
            vm((256, 128), BF),
            vm((128, 256), BF),
            vm((1024, 128), F32),
            vm((1024, 128), F32),
            vm((1024, 128), F32),
            vm((16, 64, 128), F32),
            vm((16, 64, 128), F32),
            vm((2048, 256), BF),
            vm((64, 8, 128), BF),
            vm((4, 64, 8, 128), BF),
            vm((1024, 512), BF),
            vm((64, 16, 128), BF),
            vm((64, 16, 128), BF),
            vm((64, 16, 128), BF),
            vm((64, 16, 128), BF),
            vm((128, 2048), BF),
            vm((32, 8, 128), F32),
            vm((64, 8, 128), F32),
            vm((4, 8, 128), F32),
            vm((32, 8, 128), F32),
            pltpu.SemaphoreType.DMA((2,)),
            pltpu.SemaphoreType.DMA((7,)),
            pltpu.SemaphoreType.DMA((7,)),
        ],
        compiler_params=pltpu.CompilerParams(collective_id=0, has_side_effects=True),
    )(pair, cotangent, w_left.T, w_left_gate.T, w_right.T, w_right_gate.T)
    return pg, g_l.T, g_lg.T, g_r.T, g_rg.T


def solution(mesh):
    in_specs = (P("row", "col", None), P(None, "row", "col"), P(), P(), P(), P())
    out_specs = (P("row", "col", None), P(), P(), P(), P())
    return jax.shard_map(shards, mesh=mesh, in_specs=in_specs, out_specs=out_specs, check_vma=False)
```

time: 581 us -> 64.7 us (0.11)
  waiting for transfers between devices: 440 us -> 0 us
  blocking collectives: 79.4 us -> 0 us
  Pallas kernels: 0 us -> 59.1 us
  local copies, waits for them, and re-layouts: 27.9 us -> 4.6 us
  between operations: 14 us -> 0.65 us
  matrix products: 11.3 us -> 0 us
  other arithmetic: 6.66 us -> 0 us
    psum x1 -> x0, waiting for transfers between devices: 241 us -> none  [shards(): total_weights = lax.psum(local_weights, ('row', 'col')) / residues]
    reduce_scatter x1 -> x0, waiting for transfers between devices: 152 us -> none  [shards(): lax.psum_scatter(jnp.einsum('hij,hik->jhk', col_block, left_chan, preferr...]
    all_to_all x5 -> x0, blocking collectives: 79.4 us -> none  [the longest x1 20.8 us: shards(): lax.all_to_all(right, 'col', split_axis=0, concat_axis=2, tiled=True)]
    pallas_call x0 -> x1, Pallas kernels: none -> 59.1 us  [shards(): pl.pallas_call(kernel, out_shape=[jax.ShapeDtypeStruct((16, 64, 128), BF)...]
    all_gather x1 -> x0, waiting for transfers between devices: 47.2 us -> none  [shards(): lax.all_gather(right_chan, 'row', axis=1, tiled=True)]
    dot_general x5 -> x0, matrix products: 11.3 us -> none  [the longest x1 4.5 us: shards(): jnp.einsum('hij,hik->jhk', col_block, left_chan, preferred_element_type=j...]
    transpose x1 -> x0, local copies, waits for them, and re-layouts: 10.4 us -> none  [shards(): jnp.einsum('hij,hik->jhk', col_block, left_chan, preferred_element_type=j...]
    unnamed x22 -> x13, local copies, waits for them, and re-layouts: 11 us -> 4.6 us
  transfers between devices with their start and end apart: 3 -> 0, of which waited for: 3 -> 0; matrix products, arithmetic and copies ran while one was open for 0% -> 0% of each run, Pallas kernels for 0% -> 0%
where the time goes in v1:
time: 64.7 us; the launch traced here: 64.4 us
  Pallas kernels  59.1 us (91%)
  local copies, waits for them, and re-layouts  4.6 us (7%)
  between operations  0.65 us (1%)
    pallas_call x1, Pallas kernels, shards(): pl.pallas_call(kernel, out_shape=[jax.ShapeDtypeStruct((16, 64, 128), BF)...  59.1 us
    unnamed x13, local copies, waits for them, and re-layouts  4.6 us

profile of v1, /device:TPU:1, one launch (start us, length us, event | category | flops | bytes accessed | tf_op | source)
XLA Modules:
  0.0 64.4 jit_solution(8513080261482807879)
XLA Ops:
  0.6 59.1 %shard_map.101 = (bf16[16,64,128]{2,1,0:T(8,128)(2,1)}, f32[64,128]{1,0:T(8,128)}, f32[64,128]{1,0:T(8,128)}, f32[64,128]{1,0:T(8,128)}, f32[64,128]{1,0:T(8,128)}) custom-call(bf16[16,64,128]{2,1,0:T(8,128)(2,1)} %pair_hbm.1, bf16[64,16,64]{2,1,0:T(8,128)(2,1)} %cot_hbm.1, bf16[64,128]{1,0:T(8,128)(2,1)} %bitcast.12, bf16[64,128]{1,0:T(8,128)(2,1)} %bitcast.13, ...), custom_call_target="tpu_custom_call" | custom-call | tf_op jit(solution)/shard_map/pallas_call | solution.py:245
  59.8 0.0 copy-start.3
  59.8 1.7 %copy.16 = bf16[16,64,128]{2,1,0:T(8,128)(2,1)} copy(bf16[16,64,128]{2,1,0:T(8,128)(2,1)} %get-tuple-element.20) | data formatting | bytes 524288
  61.4 0.0 copy-done.3
  61.4 0.0 copy-start.2
  61.5 0.6 copy.17
  62.1 0.2 copy-done.2
  62.2 0.0 copy-start.1
  62.2 0.6 copy.18
  62.8 0.2 copy-done.1
  63.0 0.0 copy-start
  63.0 0.6 copy.19
  63.6 0.2 copy-done
  63.8 0.6 copy.20
Async XLA Ops:
  59.8 1.7 %copy-start.3 = (f32[64,128]{1,0:T(8,128)S(1)}, f32[64,128]{1,0:T(8,128)}, u32[]{:S(2)}) copy-start(f32[64,128]{1,0:T(8,128)} %get-tuple-element.11) | copy-start | bytes 98308
  61.4 0.8 %copy-start.2 = (f32[64,128]{1,0:T(8,128)S(1)}, f32[64,128]{1,0:T(8,128)}, u32[]{:S(2)}) copy-start(f32[64,128]{1,0:T(8,128)} %get-tuple-element.12) | copy-start | bytes 98308
  62.2 0.8 %copy-start.1 = (f32[64,128]{1,0:T(8,128)S(1)}, f32[64,128]{1,0:T(8,128)}, u32[]{:S(2)}) copy-start(f32[64,128]{1,0:T(8,128)} %get-tuple-element.13) | copy-start | bytes 98308
  63.0 0.8 %copy-start = (f32[64,128]{1,0:T(8,128)S(1)}, f32[64,128]{1,0:T(8,128)}, u32[]{:S(2)}) copy-start(f32[64,128]{1,0:T(8,128)} %get-tuple-element.14) | copy-start | bytes 98308

commit v2 on v1

--- a/solution.py
+++ b/solution.py
@@ -14,8 +14,7 @@
 
 
 def kernel(
-    pair_hbm, cot_hbm, wl, wlg, wr, wrg,
-    pg_out, o_l, o_lg, o_r, o_rg,
+    pair_hbm, cot_hbm, wl, wlg, wr, wrg, pg_out, sums_out,
     pair_v, cot_v, wst, wcat, xhat, invs, scr, s_s, f_s, nblk,
     gs, gb, gg, lrs, lrb, dsd, db, efs, ws, rb, yb, ag,
     load_sem, send_sem, recv_sem,
@@ -23,13 +22,21 @@
     row, col = lax.axis_index("row"), lax.axis_index("col")
     zhi, y = lax.div(col, 4), lax.rem(col, 4)
     me = zhi * 32 + row
-    core, chip = lax.rem(row, 2), lax.div(me, 2)
+    z, spot = zhi * 4 + lax.div(row, 8), lax.rem(row, 8)
+    place = y * 8 + spot
 
     def member(g):
         return (lax.rem(g, 32), lax.div(g, 32) * 4 + y)
 
     def other_y(d):
         return (row, zhi * 4 + lax.rem(y + d, 4))
+
+    def other_z(d):
+        t = lax.rem(z + d, 8)
+        return (lax.rem(t, 4) * 8 + spot, lax.div(t, 4) * 4 + y)
+
+    def in_plane(p):
+        return (row - spot + lax.rem(p, 8), zhi * 4 + lax.div(p, 8))
 
     def remote(src, dst, phase, device):
         return pltpu.make_async_remote_copy(
@@ -37,6 +44,15 @@
             device_id=device, device_id_type=MESH,
         )
 
+    sent = [
+        gs.at[pl.ds(0, 63)], lrs.at[pl.ds(0, 63)], gb.at[pl.ds(0, 3)], dsd.at[pl.ds(0, 63)],
+        ws.at[pl.ds(0, 31)], yb.at[pl.ds(0, 7)], ag.at[pl.ds(0, 31)],
+    ]
+
+    def drain(phases):
+        for k in phases:
+            remote(sent[k], sent[k], k, other_y(1)).wait_send()
+
     load_pair = pltpu.make_async_copy(pair_hbm, pair_v, load_sem.at[0])
     load_cot = pltpu.make_async_copy(cot_hbm, cot_v, load_sem.at[1])
     load_cot.start()
@@ -51,8 +67,13 @@
         return c
 
     lax.fori_loop(1, 64, greet, 0)
-    for d in (1, 2, 3):
-        pl.semaphore_signal(barrier, inc=1, device_id=other_y(d), device_id_type=MESH)
+
+    def greet_plane(d, c):
+        p = lax.rem(y * 8 + d, 32)
+        pl.semaphore_signal(barrier, inc=1, device_id=in_plane(p), device_id_type=MESH)
+        return c
+
+    lax.fori_loop(8, 32, greet_plane, 0)
 
     wst[0:64], wst[64:128], wst[128:192], wst[192:256] = wl[...], wlg[...], wr[...], wrg[...]
     wcat[0:64, 0:128], wcat[0:64, 128:256] = wr[...], wl[...]
@@ -101,7 +122,7 @@
 
     lax.fori_loop(0, 8, round_lr, 0)
 
-    pl.semaphore_wait(barrier, 66)
+    pl.semaphore_wait(barrier, 87)
 
     def scatter(src, dst, phase):
         def step(d, c):
@@ -149,10 +170,10 @@
     for m in range(4):
         d_l = jnp.dot(gg[128 * m : 128 * m + 128], both, preferred_element_type=F32)
         d_r = jnp.dot(gg[512 + 128 * m : 640 + 128 * m], both, preferred_element_type=F32)
-        for z in range(2):
-            lanes = slice(128 * z, 128 * z + 128)
+        for half in range(2):
+            lanes = slice(128 * half, 128 * half + 128)
             d = jnp.where(low2, d_r[:, lanes], d_l[:, lanes])
-            dsd[32 * z + 8 * m : 32 * z + 8 * m + 8] = d.reshape(8, 16, 128).astype(BF)
+            dsd[32 * half + 8 * m : 32 * half + 8 * m + 8] = d.reshape(8, 16, 128).astype(BF)
 
     scatter(dsd, db.at[me], 3)
     db[me] = dsd[me]
@@ -172,19 +193,12 @@
     ws[16:32] = wg[:, 128:256].reshape(16, 8, 128)
 
     def reduce_to(d, c):
-        t = lax.rem(chip + d, 32)
-        remote(ws.at[t], rb.at[me], 4, member(2 * t)).start()
+        p = lax.rem(place + d, 32)
+        remote(ws.at[p], rb.at[place], 4, in_plane(p)).start()
         return c
 
     lax.fori_loop(1, 32, reduce_to, 0)
-
-    @pl.when(core == 1)
-    def _():
-        remote(ws.at[chip], rb.at[me], 4, member(2 * chip)).start()
-
-    @pl.when(core == 0)
-    def _():
-        rb[me] = ws[chip]
+    rb[place] = ws[place]
 
     for b in range(8):
         part = lax.dot_general(
@@ -204,49 +218,41 @@
         pg = (dn - m1 - xh * m2) * invs[128 * b : 128 * b + 128, :]
         pg_out[2 * b : 2 * b + 2] = pg.reshape(2, 64, 128).astype(BF)
 
-    @pl.when(core == 0)
-    def _():
-        remote(rb.at[pl.ds(0, 63)], rb.at[pl.ds(0, 63)], 4, other_y(1)).wait_recv()
-        yb[y] = jnp.sum(rb[...], axis=0)
-        for d in (1, 2, 3):
-            remote(yb.at[y], yb.at[y], 5, other_y(d)).start()
-        remote(yb.at[pl.ds(0, 3)], yb.at[pl.ds(0, 3)], 5, other_y(1)).wait_recv()
-        ag[chip] = ((yb[0] + yb[1]) + (yb[2] + yb[3])) * (1.0 / 512)
-
-        def share(d, c):
-            remote(ag.at[chip], ag.at[chip], 6, member(lax.rem(me + d, 64))).start()
-            return c
-
-        lax.fori_loop(1, 64, share, 0)
-        remote(ag.at[pl.ds(0, 31)], ag.at[pl.ds(0, 31)], 6, other_y(1)).wait_recv()
-        remote(rb.at[pl.ds(0, 63)], rb.at[pl.ds(0, 63)], 6, other_y(1)).wait_send()
-        remote(yb.at[pl.ds(0, 3)], yb.at[pl.ds(0, 3)], 5, other_y(1)).wait_send()
-        remote(ws.at[pl.ds(0, 31)], ws.at[pl.ds(0, 31)], 4, other_y(1)).wait_send()
-
-    @pl.when(core == 1)
-    def _():
-        remote(ag, ag, 6, other_y(1)).wait_recv()
-        remote(ws, ws, 4, other_y(1)).wait_send()
-
-    o_r[...] = ag[0:8].reshape(64, 128)
-    o_rg[...] = ag[8:16].reshape(64, 128)
-    o_l[...] = ag[16:24].reshape(64, 128)
-    o_lg[...] = ag[24:32].reshape(64, 128)
-
-    remote(gs.at[pl.ds(0, 63)], gs.at[pl.ds(0, 63)], 0, other_y(1)).wait_send()
-    remote(lrs.at[pl.ds(0, 63)], lrs.at[pl.ds(0, 63)], 1, other_y(1)).wait_send()
-    remote(gb.at[pl.ds(0, 3)], gb.at[pl.ds(0, 3)], 2, other_y(1)).wait_send()
-    remote(dsd.at[pl.ds(0, 63)], dsd.at[pl.ds(0, 63)], 3, other_y(1)).wait_send()
+    remote(rb.at[pl.ds(0, 31)], rb.at[pl.ds(0, 31)], 4, other_y(1)).wait_recv()
+    yb[z] = jnp.sum(rb[...], axis=0)
+    for d in range(1, 8):
+        remote(yb.at[z], yb.at[z], 5, other_z(d)).start()
+    remote(yb.at[pl.ds(0, 7)], yb.at[pl.ds(0, 7)], 5, other_y(1)).wait_recv()
+    ag[place] = jnp.sum(yb[...], axis=0) * (1.0 / 512)
+
+    def share(d, c):
+        remote(ag.at[place], ag.at[place], 6, in_plane(lax.rem(place + d, 32))).start()
+        return c
+
+    lax.fori_loop(1, 32, share, 0)
+    remote(ag.at[pl.ds(0, 31)], ag.at[pl.ds(0, 31)], 6, other_y(1)).wait_recv()
+    sums_out[...] = ag[...]
+    drain(range(7))
+
+
+def deliver(pg, sums, out, *rest):
+    sem = rest[-1]
+    copies = [pltpu.make_async_copy(pg, out, sem.at[0])]
+    for k in range(4):
+        copies.append(pltpu.make_async_copy(sums.at[pl.ds(8 * k, 8)], rest[k], sem.at[k + 1]))
+    for copy in copies:
+        copy.start()
+    for copy in copies:
+        copy.wait()
 
 
 def shards(pair, cotangent, w_left, w_left_gate, w_right, w_right_gate):
     vm = pltpu.VMEM
-    grad = jax.ShapeDtypeStruct((64, 128), F32)
-    pg, g_l, g_lg, g_r, g_rg = pl.pallas_call(
+    pg, sums = pl.pallas_call(
         kernel,
-        out_shape=[jax.ShapeDtypeStruct((16, 64, 128), BF), grad, grad, grad, grad],
+        out_shape=[vm((16, 64, 128), BF), vm((32, 8, 128), F32)],
         in_specs=[pl.BlockSpec(memory_space=pl.ANY)] * 2 + [pl.BlockSpec(memory_space=vm)] * 4,
-        out_specs=[pl.BlockSpec(memory_space=vm)] * 5,
+        out_specs=[pl.BlockSpec(memory_space=vm)] * 2,
         scratch_shapes=[
             vm((16, 64, 128), BF),
             vm((64, 16, 64), BF),
@@ -267,8 +273,8 @@
             vm((64, 16, 128), BF),
             vm((128, 2048), BF),
             vm((32, 8, 128), F32),
-            vm((64, 8, 128), F32),
-            vm((4, 8, 128), F32),
+            vm((32, 8, 128), F32),
+            vm((8, 8, 128), F32),
             vm((32, 8, 128), F32),
             pltpu.SemaphoreType.DMA((2,)),
             pltpu.SemaphoreType.DMA((7,)),
@@ -276,7 +282,16 @@
         ],
         compiler_params=pltpu.CompilerParams(collective_id=0, has_side_effects=True),
     )(pair, cotangent, w_left.T, w_left_gate.T, w_right.T, w_right_gate.T)
-    return pg, g_l.T, g_lg.T, g_r.T, g_rg.T
+    keep = pltpu.with_memory_space_constraint
+    grad = jax.ShapeDtypeStruct((8, 8, 128), F32)
+    out, g_r, g_rg, g_l, g_lg = pl.pallas_call(
+        deliver,
+        out_shape=[jax.ShapeDtypeStruct((16, 64, 128), BF), grad, grad, grad, grad],
+        in_specs=[pl.BlockSpec(memory_space=vm)] * 2,
+        out_specs=[pl.BlockSpec(memory_space=pl.ANY)] * 5,
+        scratch_shapes=[pltpu.SemaphoreType.DMA((5,))],
+    )(keep(pg, vm), keep(sums, vm))
+    return (out, *(g.reshape(64, 128).T for g in (g_l, g_lg, g_r, g_rg)))
 
 
 def solution(mesh):

time: 64.7 us -> 58.5 us (0.904)
  local copies, waits for them, and re-layouts: 4.6 us -> 0 us
  Pallas kernels: 59.1 us -> 57.6 us
    unnamed x13 -> x0, local copies, waits for them, and re-layouts: 4.6 us -> none
    pallas_call x1 -> x2, Pallas kernels: 59.1 us -> 57.6 us  [the longest x1 56.8 us: shards(): pl.pallas_call(kernel, out_shape=[vm((16, 64, 128), BF), vm((32, 8, 128),...]
where the time goes in v2:
time: 58.5 us; the launch traced here: 58.2 us
  Pallas kernels  57.6 us (98%)
  between operations  0.64 us (1%)
    pallas_call x1, Pallas kernels, shards(): pl.pallas_call(kernel, out_shape=[vm((16, 64, 128), BF), vm((32, 8, 128),...  56.8 us

profile of v2, /device:TPU:1, one launch (start us, length us, event | category | flops | bytes accessed | tf_op | source)
XLA Modules:
  0.0 58.2 jit_solution(6439164589561094307)
XLA Ops:
  0.6 56.8 %shard_map.101 = (bf16[16,64,128]{2,1,0:T(8,128)(2,1)S(1)}, f32[32,8,128]{2,1,0:T(8,128)S(1)}) custom-call(bf16[16,64,128]{2,1,0:T(8,128)(2,1)} %pair_hbm.1, bf16[64,16,64]{2,1,0:T(8,128)(2,1)} %cot_hbm.1, bf16[64,128]{1,0:T(8,128)(2,1)} %bitcast.16, bf16[64,128]{1,0:T(8,128)(2,1)} %bitcast.17, bf16[64,128]{1,0:T(8,128)(2,1)} %bitcast.18, ...), custom_call_target="tpu_custom_call" | custom-call | tf_op jit(solution)/shard_map/pallas_call | solution.py:251
  57.4 0.8 %shard_map.102 = (bf16[16,64,128]{2,1,0:T(8,128)(2,1)}, f32[8,8,128]{2,1,0:T(8,128)}, f32[8,8,128]{2,1,0:T(8,128)}, f32[8,8,128]{2,1,0:T(8,128)}, f32[8,8,128]{2,1,0:T(8,128)}) custom-call(bf16[16,64,128]{2,1,0:T(8,128)(2,1)S(1)} %get-tuple-element.12.pg, f32[32,8,128]{2,1,0:T(8,128)S(1)} %get-tuple-element.13.sums), custom_call_target="tpu_custom_call" | custom-call | tf_op jit(solution)/shard_map/pallas_call | solution.py:287

commit v3 on v2

v3 whole, which is shorter than its diff:
```python
import jax
import jax.numpy as jnp
from jax import lax
from jax.experimental import pallas as pl
from jax.experimental.pallas import tpu as pltpu
from jax.sharding import PartitionSpec as P

MESH = pl.DeviceIdType.MESH
BF, F32 = jnp.bfloat16, jnp.float32

G_OWN, R_OWN, G_ALL, L_OWN, D_LEFT, D_RIGHT, W_PLANE, W_Z, W_ALL = range(9)


def swap(v):
    return pltpu.roll(v, 64, v.ndim - 1)


def kernel(
    pair_hbm, cot_hbm, wl, wlg, wr, wrg, pg_out, sums_out,
    pair_v, cot_v, wst, xhat, invs, nrm, scr, s_s, f_s,
    gs, gb, gg, rs, rb, ls, lb, mat, dls, dlb, drs, drb, efs, ws, wb, zb, ag,
    load_sem, send_sem, recv_sem, g_sem,
):
    row, col = lax.axis_index("row"), lax.axis_index("col")
    zhi, y = lax.div(col, 4), lax.rem(col, 4)
    z, spot = zhi * 4 + lax.div(row, 8), lax.rem(row, 8)
    core = lax.rem(spot, 2)
    me = z * 8 + spot
    place = y * 8 + spot
    pair_of = lax.div(place, 2)

    def member(g):
        return (lax.rem(g, 32), lax.div(g, 32) * 4 + y)

    def other_y(d):
        return (row, zhi * 4 + lax.rem(y + d, 4))

    def in_plane(p):
        return (row - spot + lax.rem(p, 8), zhi * 4 + lax.div(p, 8))

    def far_first(i):
        k = lax.div(i, 8)
        dz = 4 + (1 - 2 * lax.rem(k, 2)) * lax.div(k + 1, 2)
        e = lax.rem(i, 8) + lax.div(i, 56)
        return lax.rem(z + dz, 8) * 8 + lax.rem(spot + e, 8)

    def remote(src, dst, phase, device, arrival=None):
        return pltpu.make_async_remote_copy(
            src_ref=src, dst_ref=dst, send_sem=send_sem.at[phase],
            recv_sem=recv_sem.at[phase] if arrival is None else arrival,
            device_id=device, device_id_type=MESH,
        )

    def arrived(ref, phase, arrival=None):
        remote(ref, ref, phase, other_y(1), arrival).wait_recv()

    def scatter(src, dst, phase, arrival=None):
        def step(i, c):
            g = far_first(i)
            remote(src.at[g], dst, phase, member(g), arrival).start()
            return c

        lax.fori_loop(0, 63, step, 0)

    most = pl.ds(0, 63)
    sent = [
        gs.at[most], rs.at[most], gb.at[pl.ds(0, 3)], ls.at[most], dls.at[most], drs.at[most],
        wb.at[pl.ds(0, 31)], zb.at[pl.ds(0, 7)], wb.at[pl.ds(0, 31)],
    ]

    def drain(phases):
        for k in phases:
            remote(sent[k], sent[k], k, other_y(1)).wait_send()

    barrier = pltpu.get_barrier_semaphore()

    def greet(i, c):
        pl.semaphore_signal(
            barrier, inc=1, device_id=member(far_first(i)), device_id_type=MESH
        )
        return c

    lax.fori_loop(0, 63, greet, 0)

    def greet_plane(d, c):
        p = lax.rem(y * 8 + d, 32)
        pl.semaphore_signal(barrier, inc=1, device_id=in_plane(p), device_id_type=MESH)
        return c

    lax.fori_loop(8, 32, greet_plane, 0)

    loads = [
        pltpu.make_async_copy(cot_hbm, cot_v, load_sem.at[0]),
        pltpu.make_async_copy(pair_hbm, pair_v, load_sem.at[1]),
    ]
    for k, w in enumerate((wl, wlg, wr, wrg)):
        loads.append(pltpu.make_async_copy(w, wst.at[pl.ds(64 * k, 64)], load_sem.at[2 + k]))
    for load in loads:
        load.start()

    loads[0].wait()

    def pack(t, c):
        g = cot_v[pl.ds(t * 8, 8)].astype(F32)
        gs[pl.ds(t * 8, 8)] = jnp.concatenate([g[:, :8], g[:, 8:]], axis=-1).astype(BF)
        return c

    lax.fori_loop(0, 8, pack, 0, unroll=2)
    gb[y, me] = gs[me]
    for load in loads[1:]:
        load.wait()

    def gated(side, b, n):
        pt = lax.dot_general(
            wst[128 * side : 128 * side + 128], n, (((1,), (1,)), ((), ())),
            preferred_element_type=F32,
        )
        q, s = pt[:64], jax.nn.sigmoid(pt[64:])
        v = s * q
        s_s[side, b] = s
        f_s[side, b] = v * (1.0 - s)
        scr[side, pl.ds(b, 64, stride=8), :] = v

    def normalize(b, c):
        x = jnp.concatenate([pair_v[b], pair_v[b + 8]], axis=0).astype(F32)
        cen = x - jnp.mean(x, axis=1, keepdims=True)
        var = jnp.mean(cen * cen, axis=1, keepdims=True)
        inv = jnp.broadcast_to(1.0 / jnp.sqrt(var + 1e-05), (128, 128))
        xh = cen * inv
        n = xh.astype(BF)
        xhat[pl.ds(128 * b, 128)] = xh
        invs[pl.ds(128 * b, 128)] = inv
        nrm[pl.ds(128 * b, 128)] = n
        gated(1, b, n)
        return c

    lax.fori_loop(0, 8, normalize, 0, unroll=4)
    rs[...] = scr[1].reshape(64, 8, 128).astype(BF)
    rb[me] = rs[me]
    pl.semaphore_wait(barrier, 87)
    scatter(gs, gb.at[y, me], G_OWN, g_sem.at[z])
    scatter(rs, rb.at[me], R_OWN)

    def left_too(b, c):
        gated(0, b, nrm[pl.ds(128 * b, 128)])
        return c

    lax.fori_loop(0, 8, left_too, 0, unroll=4)
    ls[...] = scr[0].reshape(64, 8, 128).astype(BF)
    lb[me] = ls[me]
    scatter(ls, lb.at[me], L_OWN)

    def spread(zz):
        block = gb.at[y, pl.ds(zz * 8, 8)]
        for d in (1, 2, 3):
            remote(block, block, G_ALL, other_y(d)).start()

    arrived(gb.at[0, pl.ds(0, 7)], G_OWN, g_sem.at[z])
    spread(z)

    def spread_next(k, c):
        zz = lax.rem(z + 8 + (2 * lax.rem(k, 2) - 1) * lax.div(k + 1, 2), 8)
        arrived(gb.at[0, pl.ds(0, 8)], G_OWN, g_sem.at[zz])
        spread(zz)
        return c

    lax.fori_loop(1, 8, spread_next, 0)
    arrived(gb.at[pl.ds(0, 3)], G_ALL)

    low3 = lax.broadcasted_iota(jnp.int32, (8, 8, 128), 2) < 64

    def interleave(a, b):
        a, b = a.astype(F32), b.astype(F32)
        top, bottom = jnp.where(low3, a, swap(b)), jnp.where(low3, swap(a), b)
        return jnp.stack([top, bottom], axis=1).reshape(128, 128).astype(BF)

    for t in range(4):
        for q in range(4):
            src = pl.ds((q // 2) * 32 + 8 * t, 8)
            gg[t * 128 : t * 128 + 128, q * 128 : q * 128 + 128] = interleave(
                gb[2 * (q % 2), src], gb[2 * (q % 2) + 1, src]
            )

    def contract(first, got, dst):
        for t in range(4):
            mat[128 * t : 128 * t + 128] = interleave(
                got[8 * t : 8 * t + 8], got[32 + 8 * t : 40 + 8 * t]
            )
        for m in range(4):
            d = jnp.dot(
                gg[first + 128 * m : first + 128 * m + 128], mat[...],
                preferred_element_type=F32,
            ).reshape(8, 2, 8, 128)
            a, b = d[:, 0], d[:, 1]
            dst[8 * m : 8 * m + 8] = jnp.where(low3, a, swap(b)).astype(BF)
            dst[32 + 8 * m : 40 + 8 * m] = jnp.where(low3, swap(a), b).astype(BF)

    arrived(rb.at[most], R_OWN)
    contract(0, rb, dls)
    scatter(dls, dlb.at[me], D_LEFT)
    dlb[me] = dls[me]

    for t in range(4):
        for q in range(4):
            block = gg[t * 128 : t * 128 + 128, q * 128 : q * 128 + 128]
            gg[512 + q * 128 : 640 + q * 128, t * 128 : t * 128 + 128] = block.T
    arrived(lb.at[most], L_OWN)
    contract(512, lb, drs)
    scatter(drs, drb.at[me], D_RIGHT)
    drb[me] = drs[me]

    def weigh(side, got):
        scr[side] = got[...].astype(F32).reshape(512, 128)
        e, f = 128 * side, 128 * side + 64
        for b in range(8):
            d = scr[side, pl.ds(b, 64, stride=8), :]
            efs[e : e + 64, 128 * b : 128 * b + 128] = (d * s_s[side, b]).astype(BF)
            efs[f : f + 64, 128 * b : 128 * b + 128] = (d * f_s[side, b]).astype(BF)
        wg = jnp.dot(efs[e : e + 128], nrm[...], preferred_element_type=F32)
        ws[:, side] = wg.reshape(16, 8, 128)

        def reduce_to(d, c):
            p = lax.rem(pair_of + d, 16)
            remote(ws.at[p, side], wb.at[place], W_PLANE, in_plane(2 * p + side)).start()
            return c

        lax.fori_loop(1, 16, reduce_to, 0)

        @pl.when(core != side)
        def _():
            own = in_plane(2 * pair_of + side)
            remote(ws.at[pair_of, side], wb.at[place], W_PLANE, own).start()

        @pl.when(core == side)
        def _():
            wb[place] = ws[pair_of, side]

    arrived(dlb.at[most], D_LEFT)
    weigh(0, dlb)
    arrived(drb.at[most], D_RIGHT)
    weigh(1, drb)
    for b in range(8):
        dn = lax.dot_general(
            efs[:, 128 * b : 128 * b + 128], wst[...], (((0,), (0,)), ((), ())),
            preferred_element_type=F32,
        )
        xh = xhat[128 * b : 128 * b + 128, :]
        m1 = jnp.mean(dn, axis=1, keepdims=True)
        m2 = jnp.mean(dn * xh, axis=1, keepdims=True)
        pg = ((dn - m1 - xh * m2) * invs[128 * b : 128 * b + 128, :]).astype(BF)
        pg_out[b], pg_out[b + 8] = pg[:64], pg[64:]

    arrived(wb.at[pl.ds(0, 31)], W_PLANE)
    zb[z] = jnp.sum(wb[...], axis=0)
    for d in range(1, 8):
        remote(zb.at[z], zb.at[z], W_Z, member(lax.rem(me + 8 * d, 64))).start()
    arrived(zb.at[pl.ds(0, 7)], W_Z)
    ag[pair_of, core] = jnp.sum(zb[...], axis=0) * (1.0 / 512)

    def share(d, c):
        mine = ag.at[pair_of, core]
        remote(mine, mine, W_ALL, in_plane(lax.rem(place + d, 32))).start()
        return c

    lax.fori_loop(1, 32, share, 0)
    arrived(wb.at[pl.ds(0, 31)], W_ALL)
    sums_out[0:16] = ag[:, 0]
    sums_out[16:32] = ag[:, 1]
    drain(range(9))


def deliver(pg, sums, out, *rest):
    sem = rest[-1]
    copies = [pltpu.make_async_copy(pg, out, sem.at[0])]
    for k in range(4):
        copies.append(pltpu.make_async_copy(sums.at[pl.ds(8 * k, 8)], rest[k], sem.at[k + 1]))
    for copy in copies:
        copy.start()
    for copy in copies:
        copy.wait()


def shards(pair, cotangent, w_left, w_left_gate, w_right, w_right_gate):
    vm, dma = pltpu.VMEM, pltpu.SemaphoreType.DMA
    chunk = vm((64, 8, 128), BF)
    pg, sums = pl.pallas_call(
        kernel,
        out_shape=[vm((16, 64, 128), BF), vm((32, 8, 128), F32)],
        in_specs=[pl.BlockSpec(memory_space=pl.ANY)] * 6,
        out_specs=[pl.BlockSpec(memory_space=vm)] * 2,
        scratch_shapes=[
            vm((16, 64, 128), BF),
            vm((64, 16, 64), BF),
            vm((256, 128), BF),
            vm((1024, 128), F32),
            vm((1024, 128), F32),
            vm((1024, 128), BF),
            vm((2, 512, 128), F32),
            vm((2, 8, 64, 128), F32),
            vm((2, 8, 64, 128), F32),
            chunk,
            vm((4, 64, 8, 128), BF),
            vm((1024, 512), BF),
            chunk, chunk, chunk, chunk,
            vm((512, 128), BF),
            chunk, chunk, chunk, chunk,
            vm((256, 1024), BF),
            vm((16, 2, 8, 128), F32),
            vm((32, 8, 128), F32),
            vm((8, 8, 128), F32),
            vm((16, 2, 8, 128), F32),
            dma((6,)), dma((9,)), dma((9,)), dma((8,)),
        ],
        compiler_params=pltpu.CompilerParams(collective_id=0, has_side_effects=True),
    )(pair, cotangent, w_left.T, w_left_gate.T, w_right.T, w_right_gate.T)
    keep = pltpu.with_memory_space_constraint
    grad = jax.ShapeDtypeStruct((8, 8, 128), F32)
    out, *grads = pl.pallas_call(
        deliver,
        out_shape=[jax.ShapeDtypeStruct((16, 64, 128), BF), grad, grad, grad, grad],
        in_specs=[pl.BlockSpec(memory_space=vm)] * 2,
        out_specs=[pl.BlockSpec(memory_space=pl.ANY)] * 5,
        scratch_shapes=[dma((5,))],
    )(keep(pg, vm), keep(sums, vm))
    return (out, *(g.reshape(64, 128).T for g in grads))


def solution(mesh):
    in_specs = (P("row", "col", None), P(None, "row", "col"), P(), P(), P(), P())
    out_specs = (P("row", "col", None), P(), P(), P(), P())
    return jax.shard_map(shards, mesh=mesh, in_specs=in_specs, out_specs=out_specs, check_vma=False)
```

time: 58.5 us -> 52.6 us (0.90)
  Pallas kernels: 57.6 us -> 51.9 us
    pallas_call x1, Pallas kernels: 56.8 us -> 51.1 us  [shards(): pl.pallas_call(kernel, out_shape=[vm((16, 64, 128), BF), vm((32, 8, 128),...]
where the time goes in v3:
time: 52.6 us; the launch traced here: 52.5 us
  Pallas kernels  51.9 us (99%)
  between operations  0.64 us (1%)
    pallas_call x1, Pallas kernels, shards(): pl.pallas_call(kernel, out_shape=[vm((16, 64, 128), BF), vm((32, 8, 128),...  51.1 us

profile of v3, /device:TPU:1, one launch (start us, length us, event | category | flops | bytes accessed | tf_op | source)
XLA Modules:
  0.0 52.5 jit_solution(11733083633407434754)
XLA Ops:
  0.6 51.1 %shard_map.101 = (bf16[16,64,128]{2,1,0:T(8,128)(2,1)S(1)}, f32[32,8,128]{2,1,0:T(8,128)S(1)}) custom-call(bf16[16,64,128]{2,1,0:T(8,128)(2,1)} %pair_hbm.1, bf16[64,16,64]{2,1,0:T(8,128)(2,1)} %cot_hbm.1, bf16[64,128]{1,0:T(8,128)(2,1)} %bitcast.16, bf16[64,128]{1,0:T(8,128)(2,1)} %bitcast.17, bf16[64,128]{1,0:T(8,128)(2,1)} %bitcast.18, ...), custom_call_target="tpu_custom_call" | custom-call | tf_op jit(solution)/shard_map/pallas_call | solution.py:286
  51.8 0.8 %shard_map.102 = (bf16[16,64,128]{2,1,0:T(8,128)(2,1)}, f32[8,8,128]{2,1,0:T(8,128)}, f32[8,8,128]{2,1,0:T(8,128)}, f32[8,8,128]{2,1,0:T(8,128)}, f32[8,8,128]{2,1,0:T(8,128)}) custom-call(bf16[16,64,128]{2,1,0:T(8,128)(2,1)S(1)} %get-tuple-element.12.pg, f32[32,8,128]{2,1,0:T(8,128)S(1)} %get-tuple-element.13.sums), custom_call_target="tpu_custom_call" | custom-call | tf_op jit(solution)/shard_map/pallas_call | solution.py:318

commit v4 on v3

--- a/solution.py
+++ b/solution.py
@@ -19,7 +19,7 @@
     pair_hbm, cot_hbm, wl, wlg, wr, wrg, pg_out, sums_out,
     pair_v, cot_v, wst, xhat, invs, nrm, scr, s_s, f_s,
     gs, gb, gg, rs, rb, ls, lb, mat, dls, dlb, drs, drb, efs, ws, wb, zb, ag,
-    load_sem, send_sem, recv_sem, g_sem,
+    load_sem, send_sem, recv_sem, g_sem, gy_sem,
 ):
     row, col = lax.axis_index("row"), lax.axis_index("col")
     zhi, y = lax.div(col, 4), lax.rem(col, 4)
@@ -38,11 +38,29 @@
     def in_plane(p):
         return (row - spot + lax.rem(p, 8), zhi * 4 + lax.div(p, 8))
 
-    def far_first(i):
-        k = lax.div(i, 8)
-        dz = 4 + (1 - 2 * lax.rem(k, 2)) * lax.div(k + 1, 2)
-        e = lax.rem(i, 8) + lax.div(i, 56)
-        return lax.rem(z + dz, 8) * 8 + lax.rem(spot + e, 8)
+    spots = [lax.rem(spot + e, 8) for e in range(8)]
+
+    def near(k):
+        return lax.rem(z + 8 + (2 * lax.rem(k, 2) - 1) * lax.div(k + 1, 2), 8)
+
+    def far(k):
+        return lax.rem(z + 4 + (1 - 2 * lax.rem(k, 2)) * lax.div(k + 1, 2), 8)
+
+    def each_member(act, near_first=False):
+        def of_z(zz, turn):
+            r, c = lax.rem(zz, 4) * 8, lax.div(zz, 4) * 4 + y
+            for e in turn:
+                act(zz * 8 + spots[e], (r + spots[e], c))
+
+        def step(k, carry):
+            of_z(near(k + 1) if near_first else far(k), range(8))
+            return carry
+
+        if near_first:
+            of_z(z, range(1, 8))
+        lax.fori_loop(0, 7, step, 0)
+        if not near_first:
+            of_z(z, range(1, 8))
 
     def remote(src, dst, phase, device, arrival=None):
         return pltpu.make_async_remote_copy(
@@ -54,13 +72,11 @@
     def arrived(ref, phase, arrival=None):
         remote(ref, ref, phase, other_y(1), arrival).wait_recv()
 
-    def scatter(src, dst, phase, arrival=None):
-        def step(i, c):
-            g = far_first(i)
-            remote(src.at[g], dst, phase, member(g), arrival).start()
-            return c
-
-        lax.fori_loop(0, 63, step, 0)
+    def scatter(src, dst, phase, arrival=None, near_first=False):
+        def send(g, device):
+            remote(src.at[g], dst, phase, device, arrival).start()
+
+        each_member(send, near_first)
 
     most = pl.ds(0, 63)
     sent = [
@@ -74,20 +90,14 @@
 
     barrier = pltpu.get_barrier_semaphore()
 
-    def greet(i, c):
-        pl.semaphore_signal(
-            barrier, inc=1, device_id=member(far_first(i)), device_id_type=MESH
-        )
-        return c
-
-    lax.fori_loop(0, 63, greet, 0)
-
-    def greet_plane(d, c):
-        p = lax.rem(y * 8 + d, 32)
-        pl.semaphore_signal(barrier, inc=1, device_id=in_plane(p), device_id_type=MESH)
-        return c
-
-    lax.fori_loop(8, 32, greet_plane, 0)
+    def greet(device):
+        pl.semaphore_signal(barrier, inc=1, device_id=device, device_id_type=MESH)
+
+    each_member(lambda g, device: greet(device))
+
+    for d in (1, 2, 3):
+        for p in spots:
+            greet((row - spot + p, zhi * 4 + lax.rem(y + d, 4)))
 
     loads = [
         pltpu.make_async_copy(cot_hbm, cot_v, load_sem.at[0]),
@@ -138,9 +148,7 @@
     rs[...] = scr[1].reshape(64, 8, 128).astype(BF)
     rb[me] = rs[me]
     pl.semaphore_wait(barrier, 87)
-    scatter(gs, gb.at[y, me], G_OWN, g_sem.at[z])
-    scatter(rs, rb.at[me], R_OWN)
-
+    scatter(gs, gb.at[y, me], G_OWN, g_sem.at[z], near_first=True)
     def left_too(b, c):
         gated(0, b, nrm[pl.ds(128 * b, 128)])
         return c
@@ -148,25 +156,25 @@
     lax.fori_loop(0, 8, left_too, 0, unroll=4)
     ls[...] = scr[0].reshape(64, 8, 128).astype(BF)
     lb[me] = ls[me]
+    drain([G_OWN])
+    scatter(rs, rb.at[me], R_OWN)
     scatter(ls, lb.at[me], L_OWN)
 
     def spread(zz):
         block = gb.at[y, pl.ds(zz * 8, 8)]
         for d in (1, 2, 3):
-            remote(block, block, G_ALL, other_y(d)).start()
+            remote(block, block, G_ALL, other_y(d), gy_sem.at[zz]).start()
 
     arrived(gb.at[0, pl.ds(0, 7)], G_OWN, g_sem.at[z])
     spread(z)
 
     def spread_next(k, c):
-        zz = lax.rem(z + 8 + (2 * lax.rem(k, 2) - 1) * lax.div(k + 1, 2), 8)
+        zz = near(k)
         arrived(gb.at[0, pl.ds(0, 8)], G_OWN, g_sem.at[zz])
         spread(zz)
         return c
 
     lax.fori_loop(1, 8, spread_next, 0)
-    arrived(gb.at[pl.ds(0, 3)], G_ALL)
-
     low3 = lax.broadcasted_iota(jnp.int32, (8, 8, 128), 2) < 64
 
     def interleave(a, b):
@@ -174,29 +182,37 @@
         top, bottom = jnp.where(low3, a, swap(b)), jnp.where(low3, swap(a), b)
         return jnp.stack([top, bottom], axis=1).reshape(128, 128).astype(BF)
 
-    for t in range(4):
-        for q in range(4):
-            src = pl.ds((q // 2) * 32 + 8 * t, 8)
-            gg[t * 128 : t * 128 + 128, q * 128 : q * 128 + 128] = interleave(
-                gb[2 * (q % 2), src], gb[2 * (q % 2) + 1, src]
-            )
-
-    def contract(first, got, dst):
+    def join(side, got):
         for t in range(4):
-            mat[128 * t : 128 * t + 128] = interleave(
+            mat[side, 128 * t : 128 * t + 128] = interleave(
                 got[8 * t : 8 * t + 8], got[32 + 8 * t : 40 + 8 * t]
             )
+
+    def contract(side, first, dst):
         for m in range(4):
             d = jnp.dot(
-                gg[first + 128 * m : first + 128 * m + 128], mat[...],
+                gg[first + 128 * m : first + 128 * m + 128], mat[side],
                 preferred_element_type=F32,
             ).reshape(8, 2, 8, 128)
             a, b = d[:, 0], d[:, 1]
             dst[8 * m : 8 * m + 8] = jnp.where(low3, a, swap(b)).astype(BF)
             dst[32 + 8 * m : 40 + 8 * m] = jnp.where(low3, swap(a), b).astype(BF)
 
+    def collect(k, c):
+        zz = near(k)
+        arrived(gb.at[0, pl.ds(0, 24)], G_ALL, gy_sem.at[zz])
+        rows = pl.ds(pl.multiple_of(lax.rem(zz, 4) * 128, 128), 128)
+        for q in range(2):
+            lanes = pl.ds(pl.multiple_of(lax.div(zz, 4) * 256 + q * 128, 128), 128)
+            src = pl.ds(zz * 8, 8)
+            gg[rows, lanes] = interleave(gb[2 * q, src], gb[2 * q + 1, src])
+        return c
+
+    lax.fori_loop(0, 4, collect, 0)
     arrived(rb.at[most], R_OWN)
-    contract(0, rb, dls)
+    join(1, rb)
+    lax.fori_loop(4, 8, collect, 0)
+    contract(1, 0, dls)
     scatter(dls, dlb.at[me], D_LEFT)
     dlb[me] = dls[me]
 
@@ -205,7 +221,8 @@
             block = gg[t * 128 : t * 128 + 128, q * 128 : q * 128 + 128]
             gg[512 + q * 128 : 640 + q * 128, t * 128 : t * 128 + 128] = block.T
     arrived(lb.at[most], L_OWN)
-    contract(512, lb, drs)
+    join(0, lb)
+    contract(0, 512, drs)
     scatter(drs, drb.at[me], D_RIGHT)
     drb[me] = drs[me]
 
@@ -266,7 +283,7 @@
     arrived(wb.at[pl.ds(0, 31)], W_ALL)
     sums_out[0:16] = ag[:, 0]
     sums_out[16:32] = ag[:, 1]
-    drain(range(9))
+    drain(range(R_OWN, 9))
 
 
 def deliver(pg, sums, out, *rest):
@@ -302,14 +319,14 @@
             vm((4, 64, 8, 128), BF),
             vm((1024, 512), BF),
             chunk, chunk, chunk, chunk,
-            vm((512, 128), BF),
+            vm((2, 512, 128), BF),
             chunk, chunk, chunk, chunk,
             vm((256, 1024), BF),
             vm((16, 2, 8, 128), F32),
             vm((32, 8, 128), F32),
             vm((8, 8, 128), F32),
             vm((16, 2, 8, 128), F32),
-            dma((6,)), dma((9,)), dma((9,)), dma((8,)),
+            dma((6,)), dma((9,)), dma((9,)), dma((8,)), dma((8,)),
         ],
         compiler_params=pltpu.CompilerParams(collective_id=0, has_side_effects=True),
     )(pair, cotangent, w_left.T, w_left_gate.T, w_right.T, w_right_gate.T)

time: 52.6 us -> 49.3 us (0.937)
  Pallas kernels: 51.9 us -> 48.6 us
    pallas_call x1, Pallas kernels: 51.1 us -> 47.8 us  [shards(): pl.pallas_call(kernel, out_shape=[vm((16, 64, 128), BF), vm((32, 8, 128),...]
where the time goes in v4:
time: 49.3 us; the launch traced here: 49.2 us
  Pallas kernels  48.6 us (99%)
  between operations  0.64 us (1%)
    pallas_call x1, Pallas kernels, shards(): pl.pallas_call(kernel, out_shape=[vm((16, 64, 128), BF), vm((32, 8, 128),...  47.8 us

profile of v4, /device:TPU:1, one launch (start us, length us, event | category | flops | bytes accessed | tf_op | source)
XLA Modules:
  0.0 49.2 jit_solution(17510391612286474258)
XLA Ops:
  0.6 47.8 %shard_map.101 = (bf16[16,64,128]{2,1,0:T(8,128)(2,1)S(1)}, f32[32,8,128]{2,1,0:T(8,128)S(1)}) custom-call(bf16[16,64,128]{2,1,0:T(8,128)(2,1)} %pair_hbm.1, bf16[64,16,64]{2,1,0:T(8,128)(2,1)} %cot_hbm.1, bf16[64,128]{1,0:T(8,128)(2,1)} %bitcast.16, bf16[64,128]{1,0:T(8,128)(2,1)} %bitcast.17, bf16[64,128]{1,0:T(8,128)(2,1)} %bitcast.18, ...), custom_call_target="tpu_custom_call" | custom-call | tf_op jit(solution)/shard_map/pallas_call | solution.py:303
  48.5 0.8 %shard_map.102 = (bf16[16,64,128]{2,1,0:T(8,128)(2,1)}, f32[8,8,128]{2,1,0:T(8,128)}, f32[8,8,128]{2,1,0:T(8,128)}, f32[8,8,128]{2,1,0:T(8,128)}, f32[8,8,128]{2,1,0:T(8,128)}) custom-call(bf16[16,64,128]{2,1,0:T(8,128)(2,1)S(1)} %get-tuple-element.12.pg, f32[32,8,128]{2,1,0:T(8,128)S(1)} %get-tuple-element.13.sums), custom_call_target="tpu_custom_call" | custom-call | tf_op jit(solution)/shard_map/pallas_call | solution.py:335

commit v5 on v4

--- a/solution.py
+++ b/solution.py
@@ -43,24 +43,27 @@
     def near(k):
         return lax.rem(z + 8 + (2 * lax.rem(k, 2) - 1) * lax.div(k + 1, 2), 8)
 
+    def paired(k):
+        return lax.rem(near(lax.div(k, 2)) + 4 * lax.rem(k, 2), 8)
+
     def far(k):
         return lax.rem(z + 4 + (1 - 2 * lax.rem(k, 2)) * lax.div(k + 1, 2), 8)
 
-    def each_member(act, near_first=False):
-        def of_z(zz, turn):
-            r, c = lax.rem(zz, 4) * 8, lax.div(zz, 4) * 4 + y
-            for e in turn:
-                act(zz * 8 + spots[e], (r + spots[e], c))
-
+    def of_z(act, zz, turn):
+        r, c = lax.rem(zz, 4) * 8, lax.div(zz, 4) * 4 + y
+        for e in turn:
+            act(zz * 8 + spots[e], (r + spots[e], c))
+
+    def each_member(act, pairs=False):
         def step(k, carry):
-            of_z(near(k + 1) if near_first else far(k), range(8))
+            of_z(act, paired(k + 1) if pairs else far(k), range(8))
             return carry
 
-        if near_first:
-            of_z(z, range(1, 8))
+        if pairs:
+            of_z(act, z, range(1, 8))
         lax.fori_loop(0, 7, step, 0)
-        if not near_first:
-            of_z(z, range(1, 8))
+        if not pairs:
+            of_z(act, z, range(1, 8))
 
     def remote(src, dst, phase, device, arrival=None):
         return pltpu.make_async_remote_copy(
@@ -72,11 +75,11 @@
     def arrived(ref, phase, arrival=None):
         remote(ref, ref, phase, other_y(1), arrival).wait_recv()
 
-    def scatter(src, dst, phase, arrival=None, near_first=False):
+    def scatter(src, dst, phase, arrival=None, pairs=False):
         def send(g, device):
             remote(src.at[g], dst, phase, device, arrival).start()
 
-        each_member(send, near_first)
+        each_member(send, pairs)
 
     most = pl.ds(0, 63)
     sent = [
@@ -90,14 +93,21 @@
 
     barrier = pltpu.get_barrier_semaphore()
 
+    chips = [lax.rem(lax.div(spot, 2) + d, 4) for d in range(4)]
+    ys = [lax.rem(y + d, 4) for d in range(4)]
+    hops = {0: 0, 1: 1, 2: 2, 3: 1}
+    around = sorted(
+        ((d, e) for d in range(4) for e in range(8)), key=lambda t: -hops[t[0]] - hops[t[1] // 2]
+    )
+
     def greet(device):
         pl.semaphore_signal(barrier, inc=1, device_id=device, device_id_type=MESH)
 
     each_member(lambda g, device: greet(device))
 
-    for d in (1, 2, 3):
-        for p in spots:
-            greet((row - spot + p, zhi * 4 + lax.rem(y + d, 4)))
+    for d, e in around:
+        if d:
+            greet((row - spot + spots[e], zhi * 4 + ys[d]))
 
     loads = [
         pltpu.make_async_copy(cot_hbm, cot_v, load_sem.at[0]),
@@ -147,8 +157,7 @@
     lax.fori_loop(0, 8, normalize, 0, unroll=4)
     rs[...] = scr[1].reshape(64, 8, 128).astype(BF)
     rb[me] = rs[me]
-    pl.semaphore_wait(barrier, 87)
-    scatter(gs, gb.at[y, me], G_OWN, g_sem.at[z], near_first=True)
+
     def left_too(b, c):
         gated(0, b, nrm[pl.ds(128 * b, 128)])
         return c
@@ -156,20 +165,21 @@
     lax.fori_loop(0, 8, left_too, 0, unroll=4)
     ls[...] = scr[0].reshape(64, 8, 128).astype(BF)
     lb[me] = ls[me]
-    drain([G_OWN])
+    pl.semaphore_wait(barrier, 87)
+    scatter(gs, gb.at[y, me], G_OWN, g_sem.at[z], pairs=True)
     scatter(rs, rb.at[me], R_OWN)
     scatter(ls, lb.at[me], L_OWN)
 
     def spread(zz):
         block = gb.at[y, pl.ds(zz * 8, 8)]
-        for d in (1, 2, 3):
+        for d in (2, 1, 3):
             remote(block, block, G_ALL, other_y(d), gy_sem.at[zz]).start()
 
     arrived(gb.at[0, pl.ds(0, 7)], G_OWN, g_sem.at[z])
     spread(z)
 
     def spread_next(k, c):
-        zz = near(k)
+        zz = paired(k)
         arrived(gb.at[0, pl.ds(0, 8)], G_OWN, g_sem.at[zz])
         spread(zz)
         return c
@@ -188,42 +198,47 @@
                 got[8 * t : 8 * t + 8], got[32 + 8 * t : 40 + 8 * t]
             )
 
-    def contract(side, first, dst):
-        for m in range(4):
-            d = jnp.dot(
-                gg[first + 128 * m : first + 128 * m + 128], mat[side],
-                preferred_element_type=F32,
-            ).reshape(8, 2, 8, 128)
-            a, b = d[:, 0], d[:, 1]
-            dst[8 * m : 8 * m + 8] = jnp.where(low3, a, swap(b)).astype(BF)
-            dst[32 + 8 * m : 40 + 8 * m] = jnp.where(low3, swap(a), b).astype(BF)
-
-    def collect(k, c):
-        zz = near(k)
+    def contract(side, first, dst, zl):
+        rows = pl.ds(pl.multiple_of(first + zl * 128, 128), 128)
+        d = jnp.dot(gg[rows], mat[side], preferred_element_type=F32).reshape(8, 2, 8, 128)
+        a, b = d[:, 0], d[:, 1]
+        dst[pl.ds(8 * zl, 8)] = jnp.where(low3, a, swap(b)).astype(BF)
+        dst[pl.ds(8 * zl + 32, 8)] = jnp.where(low3, swap(a), b).astype(BF)
+
+    def collect(k):
+        zz = paired(k)
         arrived(gb.at[0, pl.ds(0, 24)], G_ALL, gy_sem.at[zz])
-        rows = pl.ds(pl.multiple_of(lax.rem(zz, 4) * 128, 128), 128)
+        src = pl.ds(zz * 8, 8)
+        zl, half = lax.rem(zz, 4) * 128, lax.div(zz, 4) * 256
         for q in range(2):
-            lanes = pl.ds(pl.multiple_of(lax.div(zz, 4) * 256 + q * 128, 128), 128)
-            src = pl.ds(zz * 8, 8)
-            gg[rows, lanes] = interleave(gb[2 * q, src], gb[2 * q + 1, src])
-        return c
-
-    lax.fori_loop(0, 4, collect, 0)
-    arrived(rb.at[most], R_OWN)
-    join(1, rb)
-    lax.fori_loop(4, 8, collect, 0)
-    contract(1, 0, dls)
-    scatter(dls, dlb.at[me], D_LEFT)
+            block = interleave(gb[2 * q, src], gb[2 * q + 1, src])
+            i = pl.multiple_of(zl, 128)
+            j = pl.multiple_of(half + q * 128, 128)
+            gg[pl.ds(i, 128), pl.ds(j, 128)] = block
+            gg[pl.ds(512 + j, 128), pl.ds(i, 128)] = block.T
+
+    def give_back(src, dst, phase, p):
+        def send(g, device):
+            remote(src.at[g], dst, phase, device).start()
+
+        of_z(send, paired(2 * p), range(1 if p == 0 else 0, 8))
+        of_z(send, paired(2 * p + 1), range(8))
+
+    for p in range(4):
+        if p == 1:
+            arrived(lb.at[most], L_OWN)
+            join(0, lb)
+        collect(2 * p)
+        collect(2 * p + 1)
+        if p == 0:
+            arrived(rb.at[most], R_OWN)
+            join(1, rb)
+        contract(1, 0, dls, lax.rem(near(p), 4))
+        give_back(dls, dlb.at[me], D_LEFT, p)
     dlb[me] = dls[me]
-
-    for t in range(4):
-        for q in range(4):
-            block = gg[t * 128 : t * 128 + 128, q * 128 : q * 128 + 128]
-            gg[512 + q * 128 : 640 + q * 128, t * 128 : t * 128 + 128] = block.T
-    arrived(lb.at[most], L_OWN)
-    join(0, lb)
-    contract(0, 512, drs)
-    scatter(drs, drb.at[me], D_RIGHT)
+    for p in range(4):
+        contract(0, 512, drs, lax.rem(near(p), 4))
+        give_back(drs, drb.at[me], D_RIGHT, p)
     drb[me] = drs[me]
 
     def weigh(side, got):
@@ -236,12 +251,11 @@
         wg = jnp.dot(efs[e : e + 128], nrm[...], preferred_element_type=F32)
         ws[:, side] = wg.reshape(16, 8, 128)
 
-        def reduce_to(d, c):
-            p = lax.rem(pair_of + d, 16)
-            remote(ws.at[p, side], wb.at[place], W_PLANE, in_plane(2 * p + side)).start()
-            return c
-
-        lax.fori_loop(1, 16, reduce_to, 0)
+        for d, e in around:
+            if e % 2 == 0 and d + e:
+                p = ys[d] * 4 + chips[e // 2]
+                to = (row - spot + 2 * chips[e // 2] + side, zhi * 4 + ys[d])
+                remote(ws.at[p, side], wb.at[place], W_PLANE, to).start()
 
         @pl.when(core != side)
         def _():
@@ -269,21 +283,20 @@
 
     arrived(wb.at[pl.ds(0, 31)], W_PLANE)
     zb[z] = jnp.sum(wb[...], axis=0)
-    for d in range(1, 8):
+    for d in (4, 3, 5, 2, 6, 1, 7):
         remote(zb.at[z], zb.at[z], W_Z, member(lax.rem(me + 8 * d, 64))).start()
     arrived(zb.at[pl.ds(0, 7)], W_Z)
     ag[pair_of, core] = jnp.sum(zb[...], axis=0) * (1.0 / 512)
 
-    def share(d, c):
-        mine = ag.at[pair_of, core]
-        remote(mine, mine, W_ALL, in_plane(lax.rem(place + d, 32))).start()
-        return c
-
-    lax.fori_loop(1, 32, share, 0)
+    mine = ag.at[pair_of, core]
+    for d, e in around:
+        if d + e:
+            to = (row - spot + spots[e], zhi * 4 + ys[d])
+            remote(mine, mine, W_ALL, to).start()
     arrived(wb.at[pl.ds(0, 31)], W_ALL)
     sums_out[0:16] = ag[:, 0]
     sums_out[16:32] = ag[:, 1]
-    drain(range(R_OWN, 9))
+    drain(range(9))
 
 
 def deliver(pg, sums, out, *rest):

time: 49.3 us -> 48.4 us (0.982)
  Pallas kernels: 48.6 us -> 47.7 us
    pallas_call x1, Pallas kernels: 47.8 us -> 46.9 us  [shards(): pl.pallas_call(kernel, out_shape=[vm((16, 64, 128), BF), vm((32, 8, 128),...]
where the time goes in v5:
time: 48.4 us; the launch traced here: 48.3 us
  Pallas kernels  47.7 us (99%)
  between operations  0.64 us (1%)
    pallas_call x1, Pallas kernels, shards(): pl.pallas_call(kernel, out_shape=[vm((16, 64, 128), BF), vm((32, 8, 128),...  46.9 us

profile of v5, /device:TPU:1, one launch (start us, length us, event | category | flops | bytes accessed | tf_op | source)
XLA Modules:
  0.0 48.3 jit_solution(6846679559076817335)
XLA Ops:
  0.6 46.9 %shard_map.101 = (bf16[16,64,128]{2,1,0:T(8,128)(2,1)S(1)}, f32[32,8,128]{2,1,0:T(8,128)S(1)}) custom-call(bf16[16,64,128]{2,1,0:T(8,128)(2,1)} %pair_hbm.1, bf16[64,16,64]{2,1,0:T(8,128)(2,1)} %cot_hbm.1, bf16[64,128]{1,0:T(8,128)(2,1)} %bitcast.16, bf16[64,128]{1,0:T(8,128)(2,1)} %bitcast.17, bf16[64,128]{1,0:T(8,128)(2,1)} %bitcast.18, ...), custom_call_target="tpu_custom_call" | custom-call | tf_op jit(solution)/shard_map/pallas_call | solution.py:316
  47.5 0.8 %shard_map.102 = (bf16[16,64,128]{2,1,0:T(8,128)(2,1)}, f32[8,8,128]{2,1,0:T(8,128)}, f32[8,8,128]{2,1,0:T(8,128)}, f32[8,8,128]{2,1,0:T(8,128)}, f32[8,8,128]{2,1,0:T(8,128)}) custom-call(bf16[16,64,128]{2,1,0:T(8,128)(2,1)S(1)} %get-tuple-element.12.pg, f32[32,8,128]{2,1,0:T(8,128)S(1)} %get-tuple-element.13.sums), custom_call_target="tpu_custom_call" | custom-call | tf_op jit(solution)/shard_map/pallas_call | solution.py:348

commit v6 on v5

--- a/solution.py
+++ b/solution.py
@@ -91,24 +91,6 @@
         for k in phases:
             remote(sent[k], sent[k], k, other_y(1)).wait_send()
 
-    barrier = pltpu.get_barrier_semaphore()
-
-    chips = [lax.rem(lax.div(spot, 2) + d, 4) for d in range(4)]
-    ys = [lax.rem(y + d, 4) for d in range(4)]
-    hops = {0: 0, 1: 1, 2: 2, 3: 1}
-    around = sorted(
-        ((d, e) for d in range(4) for e in range(8)), key=lambda t: -hops[t[0]] - hops[t[1] // 2]
-    )
-
-    def greet(device):
-        pl.semaphore_signal(barrier, inc=1, device_id=device, device_id_type=MESH)
-
-    each_member(lambda g, device: greet(device))
-
-    for d, e in around:
-        if d:
-            greet((row - spot + spots[e], zhi * 4 + ys[d]))
-
     loads = [
         pltpu.make_async_copy(cot_hbm, cot_v, load_sem.at[0]),
         pltpu.make_async_copy(pair_hbm, pair_v, load_sem.at[1]),
@@ -117,6 +99,24 @@
         loads.append(pltpu.make_async_copy(w, wst.at[pl.ds(64 * k, 64)], load_sem.at[2 + k]))
     for load in loads:
         load.start()
+
+    barrier = pltpu.get_barrier_semaphore()
+
+    chips = [lax.rem(lax.div(spot, 2) + d, 4) for d in range(4)]
+    ys = [lax.rem(y + d, 4) for d in range(4)]
+    hops = {0: 0, 1: 1, 2: 2, 3: 1}
+    around = sorted(
+        ((d, e) for d in range(4) for e in range(8)), key=lambda t: -hops[t[0]] - hops[t[1] // 2]
+    )
+
+    def greet(device):
+        pl.semaphore_signal(barrier, inc=1, device_id=device, device_id_type=MESH)
+
+    each_member(lambda g, device: greet(device))
+
+    for d, e in around:
+        if d:
+            greet((row - spot + spots[e], zhi * 4 + ys[d]))
 
     loads[0].wait()
 
@@ -167,8 +167,8 @@
     lb[me] = ls[me]
     pl.semaphore_wait(barrier, 87)
     scatter(gs, gb.at[y, me], G_OWN, g_sem.at[z], pairs=True)
-    scatter(rs, rb.at[me], R_OWN)
-    scatter(ls, lb.at[me], L_OWN)
+    scatter(rs, rb.at[me], R_OWN, pairs=True)
+    scatter(ls, lb.at[me], L_OWN, pairs=True)
 
     def spread(zz):
         block = gb.at[y, pl.ds(zz * 8, 8)]
@@ -236,9 +236,11 @@
         contract(1, 0, dls, lax.rem(near(p), 4))
         give_back(dls, dlb.at[me], D_LEFT, p)
     dlb[me] = dls[me]
-    for p in range(4):
-        contract(0, 512, drs, lax.rem(near(p), 4))
-        give_back(drs, drb.at[me], D_RIGHT, p)
+    d = jnp.dot(gg[512:], mat[0], preferred_element_type=F32).reshape(32, 2, 8, 128)
+    low4 = lax.broadcasted_iota(jnp.int32, (32, 8, 128), 2) < 64
+    drs[0:32] = jnp.where(low4, d[:, 0], swap(d[:, 1])).astype(BF)
+    drs[32:64] = jnp.where(low4, swap(d[:, 0]), d[:, 1]).astype(BF)
+    scatter(drs, drb.at[me], D_RIGHT)
     drb[me] = drs[me]
 
     def weigh(side, got):

time: 48.4 us -> 48.2 us (level)
  no operation moved by 1% of the time
where the time goes in v6:
time: 48.2 us; the launch traced here: 48.1 us
  Pallas kernels  47.5 us (99%)
  between operations  0.64 us (1%)
    pallas_call x1, Pallas kernels, shards(): pl.pallas_call(kernel, out_shape=[vm((16, 64, 128), BF), vm((32, 8, 128),...  46.7 us

profile of v6, /device:TPU:1, one launch (start us, length us, event | category | flops | bytes accessed | tf_op | source)
XLA Modules:
  0.0 48.1 jit_solution(17560642489233729299)
XLA Ops:
  0.6 46.7 %shard_map.101 = (bf16[16,64,128]{2,1,0:T(8,128)(2,1)S(1)}, f32[32,8,128]{2,1,0:T(8,128)S(1)}) custom-call(bf16[16,64,128]{2,1,0:T(8,128)(2,1)} %pair_hbm.1, bf16[64,16,64]{2,1,0:T(8,128)(2,1)} %cot_hbm.1, bf16[64,128]{1,0:T(8,128)(2,1)} %bitcast.16, bf16[64,128]{1,0:T(8,128)(2,1)} %bitcast.17, bf16[64,128]{1,0:T(8,128)(2,1)} %bitcast.18, ...), custom_call_target="tpu_custom_call" | custom-call | tf_op jit(solution)/shard_map/pallas_call | solution.py:318
  47.3 0.8 %shard_map.102 = (bf16[16,64,128]{2,1,0:T(8,128)(2,1)}, f32[8,8,128]{2,1,0:T(8,128)}, f32[8,8,128]{2,1,0:T(8,128)}, f32[8,8,128]{2,1,0:T(8,128)}, f32[8,8,128]{2,1,0:T(8,128)}) custom-call(bf16[16,64,128]{2,1,0:T(8,128)(2,1)S(1)} %get-tuple-element.12.pg, f32[32,8,128]{2,1,0:T(8,128)S(1)} %get-tuple-element.13.sums), custom_call_target="tpu_custom_call" | custom-call | tf_op jit(solution)/shard_map/pallas_call | solution.py:350

commit v7 on v6

--- a/solution.py
+++ b/solution.py
@@ -272,7 +272,7 @@
     weigh(0, dlb)
     arrived(drb.at[most], D_RIGHT)
     weigh(1, drb)
-    for b in range(8):
+    for b in range(4):
         dn = lax.dot_general(
             efs[:, 128 * b : 128 * b + 128], wst[...], (((0,), (0,)), ((), ())),
             preferred_element_type=F32,
@@ -287,6 +287,17 @@
     zb[z] = jnp.sum(wb[...], axis=0)
     for d in (4, 3, 5, 2, 6, 1, 7):
         remote(zb.at[z], zb.at[z], W_Z, member(lax.rem(me + 8 * d, 64))).start()
+    for b in range(4, 8):
+        dn = lax.dot_general(
+            efs[:, 128 * b : 128 * b + 128], wst[...], (((0,), (0,)), ((), ())),
+            preferred_element_type=F32,
+        )
+        xh = xhat[128 * b : 128 * b + 128, :]
+        m1 = jnp.mean(dn, axis=1, keepdims=True)
+        m2 = jnp.mean(dn * xh, axis=1, keepdims=True)
+        pg = ((dn - m1 - xh * m2) * invs[128 * b : 128 * b + 128, :]).astype(BF)
+        pg_out[b], pg_out[b + 8] = pg[:64], pg[64:]
+
     arrived(zb.at[pl.ds(0, 7)], W_Z)
     ag[pair_of, core] = jnp.sum(zb[...], axis=0) * (1.0 / 512)
 

time: 48.2 us -> 48.2 us (level)
  no operation moved by 1% of the time
where the time goes in v7:
time: 48.2 us; the launch traced here: 48.1 us
  Pallas kernels  47.5 us (99%)
  between operations  0.64 us (1%)
    pallas_call x1, Pallas kernels, shards(): pl.pallas_call(kernel, out_shape=[vm((16, 64, 128), BF), vm((32, 8, 128),...  46.7 us

profile of v7, /device:TPU:1, one launch (start us, length us, event | category | flops | bytes accessed | tf_op | source)
XLA Modules:
  0.0 48.1 jit_solution(18249920604989641378)
XLA Ops:
  0.6 46.7 %shard_map.101 = (bf16[16,64,128]{2,1,0:T(8,128)(2,1)S(1)}, f32[32,8,128]{2,1,0:T(8,128)S(1)}) custom-call(bf16[16,64,128]{2,1,0:T(8,128)(2,1)} %pair_hbm.1, bf16[64,16,64]{2,1,0:T(8,128)(2,1)} %cot_hbm.1, bf16[64,128]{1,0:T(8,128)(2,1)} %bitcast.16, bf16[64,128]{1,0:T(8,128)(2,1)} %bitcast.17, bf16[64,128]{1,0:T(8,128)(2,1)} %bitcast.18, ...), custom_call_target="tpu_custom_call" | custom-call | tf_op jit(solution)/shard_map/pallas_call | solution.py:329
  47.3 0.8 %shard_map.102 = (bf16[16,64,128]{2,1,0:T(8,128)(2,1)}, f32[8,8,128]{2,1,0:T(8,128)}, f32[8,8,128]{2,1,0:T(8,128)}, f32[8,8,128]{2,1,0:T(8,128)}, f32[8,8,128]{2,1,0:T(8,128)}) custom-call(bf16[16,64,128]{2,1,0:T(8,128)(2,1)S(1)} %get-tuple-element.12.pg, f32[32,8,128]{2,1,0:T(8,128)S(1)} %get-tuple-element.13.sums), custom_call_target="tpu_custom_call" | custom-call | tf_op jit(solution)/shard_map/pallas_call | solution.py:361
